TPU v7x, 256 devices: a whole 4x4x8 slice. The times are simulated.
256 devices in a mesh: ctx: 32 (over y_hi, z, core), exp: 8 (over x, y_lo).
Axes of the slice: x: 4, y: 4 (y_hi: 2, y_lo: 2; y = y_hi * 2 + y_lo), z: 8, core: 2. Of those that a mesh axis runs over, the one named last changes fastest.
Arguments:
- queries: bfloat16 [4096, 6144], P('ctx', 'exp'), may hold values from -12 to 12
- keys_values: bfloat16 [4096, 8, 256], P('ctx', 'exp'), may hold values from -12 to 12
- doc_ids: int32 [4096], P('ctx'), may hold values from 0 to 7, never falling along the last dimension, each value on 1 to 3072 neighbouring positions
- gate_up: bfloat16 [8, 1280, 16384], P('exp', None, 'ctx'), may hold values from -6 to 6
- down_weight: bfloat16 [8, 16384, 6144], P('exp', 'ctx'), may hold values from -0.046875 to 0.046875
- routes: int32 [4096, 2], P(('ctx', 'exp')), may hold values from 0 to 7, all different within a row; in each aligned block of 16 rows (0 to 15, 16 to 31, ...) at most 5 rows name the same one
- route_weights: float32 [4096, 2], P(('ctx', 'exp')), may hold values from 0.1 to 1
Outputs:
- context: bfloat16 [4096, 6144], P('ctx', 'exp')
- moe_out: bfloat16 [4096, 6144], P(('ctx', 'exp'))
Inputs may be any that keep to these rules, and one draw needn't show every extreme that they name: doc_ids never falls along the sequence; each document has 1 to 3072 tokens and one has exactly 3072. `routes`: the 2 experts of a token differ; among the 16 tokens of one device (aligned blocks) no expert is named more than 5 times, a bound that some block reaches.
All inputs are finite; a program needn't handle non-finite values.
Results may differ from a plain program's by a relative error of at most 0.025.
Values may be sent and summed in bfloat16 or wider, within the bound.
No kernel may reach another device: no remote copies, remote signals or barrier semaphores. Data moves between devices by JAX's collectives and lax.ppermute only.
A program may use at most 128 MiB of HBM per device.

v0:
```python
import math
import jax
import jax.numpy as jnp
from jax import lax
from jax.sharding import PartitionSpec as P


def shards(queries, keys_values, doc_ids, gate_up, down_weight, routes, route_weights):
    tok_rows = queries.shape[0]
    local_heads = keys_values.shape[1]
    head_size = keys_values.shape[2] // 2
    groups = queries.shape[1] // (local_heads * head_size)
    query_grid = queries.reshape(tok_rows, local_heads, groups, head_size)
    first_pos = lax.axis_index("ctx") * tok_rows
    query_pos = first_pos + jnp.arange(tok_rows, dtype=jnp.int32)
    scale = 1.0 / math.sqrt(head_size)
    doc_wire = doc_ids.astype(jnp.bfloat16)
    kv_piece = lax.all_gather(keys_values, "ctx", axis=0, tiled=True)
    doc_piece = lax.all_gather(doc_wire, "ctx", axis=0, tiled=True)
    count = kv_piece.shape[0]
    key_pos = jnp.arange(count, dtype=jnp.int32)
    scores = (
        jnp.einsum(
            "qhgd,khd->hgqk",
            query_grid,
            kv_piece[:, :, :head_size],
            preferred_element_type=jnp.float32,
        )
        * scale
    )
    allowed = (doc_ids[:, None] == doc_piece.astype(jnp.int32)[None, :]) & (
        key_pos[None, :] <= query_pos[:, None]
    )
    scores = jnp.where(allowed, scores, jnp.float32(-1e30))
    run_max = jnp.full((local_heads, groups, tok_rows), -1e30, jnp.float32)
    new_max = jnp.maximum(run_max, jnp.max(scores, axis=-1))
    weights = jnp.where(allowed, jnp.exp(scores - new_max[..., None]), jnp.float32(0.0))
    new_total = jnp.sum(weights, axis=-1)
    update = jnp.einsum(
        "hgqk,khd->qhgd",
        weights.astype(jnp.bfloat16),
        kv_piece[:, :, head_size:],
        preferred_element_type=jnp.float32,
    )
    context = (
        (update / jnp.transpose(new_total, (2, 0, 1))[..., None])
        .reshape(tok_rows, -1)
        .astype(jnp.bfloat16)
    )
    residual = lax.all_to_all(context, "exp", split_axis=0, concat_axis=1, tiled=True)
    acts = gate_up[0]
    weight = down_weight[0]
    slot_total = acts.shape[0]
    ctx_count = lax.axis_size("ctx")
    exp_count = lax.axis_size("exp")
    capacity = slot_total // (ctx_count * exp_count)
    width = weight.shape[1]
    mine = lax.psum_scatter(
        jnp.dot(acts, weight, preferred_element_type=jnp.float32).astype(jnp.bfloat16),
        "ctx",
        scatter_dimension=0,
        tiled=True,
    ).astype(jnp.float32)
    mine = mine.astype(jnp.bfloat16).reshape(exp_count, capacity, width)
    home_rows = lax.all_to_all(mine, "exp", split_axis=0, concat_axis=0, tiled=True)
    expert_count = home_rows.shape[0]
    flat_routes = routes.reshape(-1)
    onehot = (flat_routes[:, None] == jnp.arange(expert_count, dtype=jnp.int32)[None, :]).astype(
        jnp.int32
    )
    earlier = jnp.cumsum(onehot, axis=0) - onehot
    slot_index = jnp.sum(earlier * onehot, axis=1)
    row_index = flat_routes * capacity + slot_index
    picked = home_rows.reshape(expert_count * capacity, width)[row_index]
    picked = picked.reshape(routes.shape[0], routes.shape[1], width).astype(jnp.float32)
    mixed = jnp.sum(route_weights[:, :, None] * picked, axis=1)
    moe_out = (residual.astype(jnp.float32) + mixed).astype(jnp.bfloat16)
    return (context, moe_out)


def solution(mesh):
    in_specs = (
        P("ctx", "exp"),
        P("ctx", "exp", None),
        P("ctx"),
        P("exp", None, "ctx"),
        P("exp", "ctx", None),
        P(("ctx", "exp"), None),
        P(("ctx", "exp"), None),
    )
    out_specs = (P("ctx", "exp"), P(("ctx", "exp"), None))
    return jax.shard_map(shards, mesh=mesh, in_specs=in_specs, out_specs=out_specs, check_vma=False)
```

profile of v0, /device:TPU:8, one launch (start us, length us, event | category | flops | bytes accessed | tf_op | source)
XLA Modules:
  0.0 310.8 jit_solution(5982555002560854336)
XLA Ops:
  7.2 0.0 copy-start
  7.2 0.0 all-gather.3.cloned.1.call-start
  7.2 0.7 all-gather.3.cloned.1.call-update
  7.9 0.0 reduce-scatter.2.cloned.1.call-start
  8.0 0.5 copy-done
  8.5 14.4 %convolution_convert_fusion = bf16[1280,6144]{1,0:T(8,128)(2,1)} fusion(bf16[1,512,6144]{2,1,0:T(8,128)(2,1)} %param.11, bf16[1,1280,512]{2,1,0:T(8,128)(2,1)S(1)} %copy-done), kind=kOutput, calls=%fused_computation.1 | convolution fusion | flops 8060928000 | bytes 23330816 | tf_op jit(solution)/shard_map/dot_general | solution.py:59
  22.9 0.0 copy-start.4
  22.9 0.0 copy-start.1
  22.9 0.0 copy-start.2
  22.9 0.0 reduce-scatter.2.cloned.1.call-update
  23.0 0.6 copy-done.4
  23.6 43.7 %all-gather = bf16[32,1,128]{2,1,0:T(2,128)(2,1)S(1)} all-gather(bf16[1,1,128]{2,1,0:T(2,128)(2,1)S(1)} %convert_bitcast_fusion.1), channel_id=1, replica_groups=mesh['ctx'=32,'exp'=8] {'ctx'}, dimensions={0}, use_global_device_ids=true | all-gather | bytes 8448 | tf_op jit(solution)/shard_map/all_gather | solution.py:19
  67.4 0.0 copy-done.1
  67.4 0.2 copy.36
  67.5 0.0 copy-done.2
  67.5 0.1 copy.44
  67.6 0.1 eq.31
  67.7 0.1 fusion.20
  67.8 1.8 fusion.8
  69.7 23.1 %all-gather.3.cloned.1.call-done = bf16[4096,1,256]{2,0,1:T(8,128)(2,1)} async-done(((bf16[128,1,256]{2,0,1:T(8,128)(2,1)}), bf16[4096,1,256]{2,0,1:T(8,128)(2,1)}) %all-gather.3.cloned.1.call-update) | async-done | bytes 2097168 | tf_op jit(solution)/shard_map/all_gather | solution.py:18
  92.8 0.0 copy-start.5
  92.8 3.3 %fusion = (f32[6,128]{1,0:T(8,128)S(1)}, f32[4096,128,6]{1,0,2:T(8,128)S(1)}) fusion(pred[128,4096]{0,1:T(8,128)(4,1)S(1)} %fusion.8, bf16[128,6,128]{0,2,1:T(8,128)(2,1)S(1)} %bitcast.86, bf16[4096,1,256]{2,0,1:T(8,128)(2,1)} %all-gather.3.cloned.1.call-done), kind=kOutput, calls=%fused_computation.4 | convolution fusion | flops 814742784 | bytes 14355456 | tf_op jit(solution)/shard_map/qhgd,khd->hgqk/dot_general | solution.py:23
  96.1 3.1 fusion.1
  99.2 0.0 copy-done.5
  99.2 0.0 copy-start.3
  99.3 3.4 %fusion.17 = bf16[128,1,6,128]{0,3,2,1:T(8,128)(2,1)S(1)} fusion(bf16[4096,1,256]{2,0,1:T(8,128)(2,1)S(1)} %copy-done.5, f32[4096,128,6]{1,0,2:T(8,128)S(1)} %get-tuple-element.11, f32[6,128]{1,0:T(8,128)S(1)} %broadcast_maximum_fusion, pred[128,4096]{0,1:T(8,128)(4,1)S(1)} %fusion.8, f32[128,6]{0,1:T(8,128)S(1)} %bitcast.88), kind=kOutput, calls=%fused_computation.19 | convolution fusion | flops 821231616 | bytes 14360576 | tf_op jit(solution)/shard_map/hgqk,khd->qhgd/dot_general | solution.py:39
  102.6 0.2 copy.40
  102.8 0.9 convert_element_type.50
  103.8 5.7 %all-to-all-start = ((bf16[8,16,768]{2,1,0:T(8,128)(2,1)}), bf16[8,16,768]{2,1,0:T(8,128)(2,1)S(1)}, u32[]{:S(2)}, u32[]{:S(2)}) async-start(bf16[8,16,768]{2,1,0:T(8,128)(2,1)} %convert_element_type.50), calls=%async_computation | async-start | bytes 393216 | tf_op jit(solution)/shard_map/all_to_all | solution.py:50
  109.5 0.1 copy.43
  109.6 0.1 mul.50
  109.6 0.1 reduce_window_sum.11
  109.7 0.2 select_reduce_fusion
  109.9 173.7 %reduce-scatter.2.cloned.1.call-done = bf16[40,6144]{1,0:T(8,128)(2,1)} async-done(((bf16[1280,6144]{1,0:T(8,128)(2,1)}), bf16[40,6144]{1,0:T(8,128)(2,1)}) %reduce-scatter.2.cloned.1.call-update) | async-done | bytes 491536 | tf_op jit(solution)/shard_map/reduce_scatter | solution.py:58
  283.6 2.1 reshape.94
  285.7 0.0 all-to-all-done
  285.7 5.8 %all-to-all-start.1 = ((bf16[8,5,6144]{2,1,0:T(8,128)(2,1)}), bf16[8,5,6144]{2,1,0:T(8,128)(2,1)S(1)}, u32[]{:S(2)}, u32[]{:S(2)}) async-start(bf16[8,5,6144]{2,1,0:T(8,128)(2,1)} %reshape.94), calls=%async_computation.2 | async-start | bytes 1572864 | tf_op jit(solution)/shard_map/all_to_all | solution.py:65
  291.6 0.0 copy-done.3
  291.6 0.1 copy.42
  291.7 0.8 copy.45
  292.6 8.0 %all-to-all-done.1 = bf16[8,5,6144]{2,1,0:T(8,128)(2,1)S(1)} async-done(((bf16[8,5,6144]{2,1,0:T(8,128)(2,1)}), bf16[8,5,6144]{2,1,0:T(8,128)(2,1)S(1)}, u32[]{:S(2)}, u32[]{:S(2)}) %all-to-all-start.1) | async-done | bytes 491552 | tf_op jit(solution)/shard_map/all_to_all | solution.py:65
  300.6 0.2 reshape.95
  300.8 0.8 gather_fusion
  301.6 0.5 reshape.97
  302.1 1.1 multiply_reduce_fusion
  303.2 0.7 add_convert_fusion
  (9 shorter events, 0.1 us)
Async XLA Ops:
  7.2 1.3 copy-start
  7.2 85.6 %all-gather.3.cloned.1.call-start = ((), (), s32[]{:S(2)}) async-start(), calls=%async_computation.3 | async-start | bytes 2162688 | tf_op jit(solution)/shard_map/all_gather | solution.py:18
  7.9 275.7 %reduce-scatter.2.cloned.1.call-start = ((), (), s32[]{:S(2)}) async-start(), calls=%async_computation.4 | async-start | bytes 16220160 | tf_op jit(solution)/shard_map/reduce_scatter | solution.py:58
  22.9 0.7 copy-start.4
  22.9 44.4 %copy-start.1 = (bf16[128,768]{1,0:T(8,128)(2,1)S(1)}, bf16[128,768]{1,0:T(8,128)(2,1)}, u32[]{:S(2)}) copy-start(bf16[128,768]{1,0:T(8,128)(2,1)} %param.7) | copy-start | bytes 589828
  22.9 44.6 %copy-start.2 = (s32[16,2]{0,1:T(2,128)S(1)}, s32[16,2]{0,1:T(2,128)}, u32[]{:S(2)}) copy-start(s32[16,2]{0,1:T(2,128)} %param.12) | copy-start | bytes 388
  92.8 6.5 %copy-start.5 = (bf16[4096,1,256]{2,0,1:T(8,128)(2,1)S(1)}, bf16[4096,1,256]{2,0,1:T(8,128)(2,1)}, u32[]{:S(2)}) copy-start(bf16[4096,1,256]{2,0,1:T(8,128)(2,1)} %all-gather.3.cloned.1.call-done) | copy-start | bytes 6291460
  99.2 192.3 %copy-start.3 = (f32[16,2]{0,1:T(2,128)S(1)}, f32[16,2]{0,1:T(2,128)}, u32[]{:S(2)}) copy-start(f32[16,2]{0,1:T(2,128)} %param.13) | copy-start | bytes 388
  103.8 182.0 %all-to-all-start = ((bf16[8,16,768]{2,1,0:T(8,128)(2,1)}), bf16[8,16,768]{2,1,0:T(8,128)(2,1)S(1)}, u32[]{:S(2)}, u32[]{:S(2)}) async-start(bf16[8,16,768]{2,1,0:T(8,128)(2,1)} %convert_element_type.50), calls=%async_computation | async-start | bytes 393216 | tf_op jit(solution)/shard_map/all_to_all | solution.py:50
  285.7 14.9 %all-to-all-start.1 = ((bf16[8,5,6144]{2,1,0:T(8,128)(2,1)}), bf16[8,5,6144]{2,1,0:T(8,128)(2,1)S(1)}, u32[]{:S(2)}, u32[]{:S(2)}) async-start(bf16[8,5,6144]{2,1,0:T(8,128)(2,1)} %reshape.94), calls=%async_computation.2 | async-start | bytes 1572864 | tf_op jit(solution)/shard_map/all_to_all | solution.py:65
Sparse Core Ops, SparseCore 0:
  10.8 81.9 all-gather.2
  97.4 186.1 reduce-scatter.1
where the time goes:
time: 311 us
  waiting for transfers between devices  206 us (66%)
  blocking collectives  43.7 us (14%)
  matrix products  21.2 us (7%)
  between operations  14.2 us (5%)
  starting transfers between devices  11.6 us (4%)
  local copies, waits for them, and re-layouts  7.36 us (2%)
  other arithmetic  7.13 us (2%)
    reduce_scatter x1, waiting for transfers between devices, shards(): lax.psum_scatter(jnp.dot(acts, weight, preferred_element_type=jnp.float32...  174 us
    all_gather x1, blocking collectives, shards(): doc_piece = lax.all_gather(doc_wire, 'ctx', axis=0, tiled=True)  43.7 us
    all_gather x1, waiting for transfers between devices, shards(): kv_piece = lax.all_gather(keys_values, 'ctx', axis=0, tiled=True)  23.1 us
    dot_general x1, matrix products, shards(): jnp.dot(acts, weight, preferred_element_type=jnp.float32)  14.4 us
    all_to_all x1, waiting for transfers between devices, shards(): lax.all_to_all(mine, 'exp', split_axis=0, concat_axis=0, tiled=True)  8.03 us
  transfers between devices with their start and end apart: 4, of which 3 were waited for; matrix products, arithmetic and copies ran while one was open for 10% of the time, Pallas kernels for 0%

commit v1 on v0

--- a/solution.py
+++ b/solution.py
@@ -15,7 +15,9 @@
     query_pos = first_pos + jnp.arange(tok_rows, dtype=jnp.int32)
     scale = 1.0 / math.sqrt(head_size)
     doc_wire = doc_ids.astype(jnp.bfloat16)
-    kv_piece = lax.all_gather(keys_values, "ctx", axis=0, tiled=True)
+    kv_piece = jnp.concatenate(
+        lax.all_to_all(jnp.stack([keys_values] * lax.axis_size("ctx")), "ctx", 0, 0), axis=0
+    )
     doc_piece = lax.all_gather(doc_wire, "ctx", axis=0, tiled=True)
     count = kv_piece.shape[0]
     key_pos = jnp.arange(count, dtype=jnp.int32)

time: 311 us -> 242 us (0.78)
  waiting for transfers between devices: 206 us -> 84.7 us
  blocking collectives: 43.7 us -> 81.4 us
  starting transfers between devices: 11.6 us -> 22.2 us
    reduce_scatter x1, waiting for transfers between devices: 174 us -> 76.6 us  [shards(): lax.psum_scatter(jnp.dot(acts, weight, preferred_element_type=jnp.float32...]
    all_gather x1, blocking collectives: 43.7 us -> 81.4 us  [shards(): doc_piece = lax.all_gather(doc_wire, 'ctx', axis=0, tiled=True)]
    all_gather x1 -> x0, waiting for transfers between devices: 23.1 us -> none  [shards(): kv_piece = lax.all_gather(keys_values, 'ctx', axis=0, tiled=True)]
    all_to_all x0 -> x1, starting transfers between devices: none -> 10.7 us  [shards(): lax.all_to_all(jnp.stack([keys_values] * lax.axis_size('ctx')), 'ctx', 0, 0)]
  transfers between devices with their start and end apart: 4 -> 4, of which waited for: 3 -> 2; matrix products, arithmetic and copies ran while one was open for 10% -> 8% of each run, Pallas kernels for 0% -> 0%
where the time goes in v1:
time: 242 us
  waiting for transfers between devices  84.7 us (35%)
  blocking collectives  81.4 us (34%)
  matrix products  22.3 us (9%)
  starting transfers between devices  22.2 us (9%)
  between operations  14.2 us (6%)
  local copies, waits for them, and re-layouts  9.86 us (4%)
  other arithmetic  7.12 us (3%)
    all_gather x1, blocking collectives, shards(): doc_piece = lax.all_gather(doc_wire, 'ctx', axis=0, tiled=True)  81.4 us
    reduce_scatter x1, waiting for transfers between devices, shards(): lax.psum_scatter(jnp.dot(acts, weight, preferred_element_type=jnp.float32...  76.6 us
    dot_general x1, matrix products, shards(): jnp.dot(acts, weight, preferred_element_type=jnp.float32)  14.4 us
    all_to_all x1, starting transfers between devices, shards(): lax.all_to_all(jnp.stack([keys_values] * lax.axis_size('ctx')), 'ctx', 0, 0)  10.7 us
    all_to_all x1, waiting for transfers between devices, shards(): lax.all_to_all(mine, 'exp', split_axis=0, concat_axis=0, tiled=True)  8.03 us
    all_to_all x1, starting transfers between devices, shards(): lax.all_to_all(context, 'exp', split_axis=0, concat_axis=1, tiled=True)  5.75 us
    all_to_all x1, starting transfers between devices, shards(): lax.all_to_all(mine, 'exp', split_axis=0, concat_axis=0, tiled=True)  5.72 us
  transfers between devices with their start and end apart: 4, of which 2 were waited for; matrix products, arithmetic and copies ran while one was open for 8% of the time, Pallas kernels for 0%

profile of v1, /device:TPU:8, one launch (start us, length us, event | category | flops | bytes accessed | tf_op | source)
XLA Modules:
  0.0 241.8 jit_solution(10525211183050746185)
XLA Ops:
  7.2 0.0 copy-start
  7.2 0.0 reduce-scatter.2.cloned.1.call-start
  7.2 1.3 copy-done
  8.5 14.4 %convolution_convert_fusion = bf16[1280,6144]{1,0:T(8,128)(2,1)} fusion(bf16[1,512,6144]{2,1,0:T(8,128)(2,1)} %param.11, bf16[1,1280,512]{2,1,0:T(8,128)(2,1)S(1)} %copy-done), kind=kOutput, calls=%fused_computation.1 | convolution fusion | flops 8060928000 | bytes 23330816 | tf_op jit(solution)/shard_map/dot_general | solution.py:61
  22.9 0.0 copy-start.2
  22.9 0.0 copy-start.5
  22.9 0.0 copy-start.1
  22.9 0.0 copy-start.3
  22.9 0.0 reduce-scatter.2.cloned.1.call-update
  23.0 0.8 copy-done.2
  23.8 1.6 stack.2
  25.4 10.7 %all-to-all-start = ((bf16[32,128,1,256]{3,1,2,0:T(8,128)(2,1)}), bf16[32,128,1,256]{3,1,2,0:T(8,128)(2,1)}, u32[]{:S(2)}, u32[]{:S(2)}) async-start(bf16[32,128,1,256]{3,1,2,0:T(8,128)(2,1)} %stack.2), calls=%async_computation | async-start | bytes 4194304 | tf_op jit(solution)/shard_map/all_to_all | solution.py:19
  36.1 0.0 copy-done.5
  36.1 81.4 %all-gather = bf16[32,1,128]{2,1,0:T(2,128)(2,1)S(1)} all-gather(bf16[1,1,128]{2,1,0:T(2,128)(2,1)S(1)} %convert_bitcast_fusion.1), channel_id=1, replica_groups=mesh['ctx'=32,'exp'=8] {'ctx'}, dimensions={0}, use_global_device_ids=true | all-gather | bytes 8448 | tf_op jit(solution)/shard_map/all_gather | solution.py:21
  117.6 0.0 copy-done.1
  117.6 0.2 copy.36
  117.8 0.0 copy-done.3
  117.8 0.1 copy.44
  117.9 0.1 eq.31
  118.0 0.1 fusion.20
  118.0 1.8 fusion.8
  119.9 0.0 all-to-all-done
  119.9 3.2 %fusion = (f32[6,128]{1,0:T(8,128)S(1)}, f32[4096,128,6]{1,0,2:T(8,128)S(1)}) fusion(pred[128,4096]{0,1:T(8,128)(4,1)S(1)} %fusion.8, bf16[128,6,128]{0,2,1:T(8,128)(2,1)S(1)} %bitcast.88, bf16[4096,1,256]{2,0,1:T(8,128)(2,1)} %bitcast.3), kind=kOutput, calls=%fused_computation.4 | convolution fusion | flops 814742784 | bytes 14355456 | tf_op jit(solution)/shard_map/qhgd,khd->hgqk/dot_general | solution.py:25
  123.1 3.1 %fusion.1 = f32[6,128]{1,0:T(8,128)S(1)} fusion(f32[4096,128,6]{1,0,2:T(8,128)S(1)} %get-tuple-element.11, f32[6,128]{1,0:T(8,128)S(1)} %broadcast_maximum_fusion, pred[128,4096]{0,1:T(8,128)(4,1)S(1)} %fusion.8), kind=kLoop, calls=%fused_computation.5 | loop fusion | flops 15727872 | bytes 13113344 | tf_op jit(solution)/shard_map/reduce_sum | solution.py:40
  126.2 0.0 copy-start.4
  126.2 4.7 %fusion.17 = bf16[128,1,6,128]{0,3,2,1:T(8,128)(2,1)S(1)} fusion(bf16[4096,1,256]{2,0,1:T(8,128)(2,1)} %bitcast.3, f32[4096,128,6]{1,0,2:T(8,128)S(1)} %get-tuple-element.11, f32[6,128]{1,0:T(8,128)S(1)} %broadcast_maximum_fusion, pred[128,4096]{0,1:T(8,128)(4,1)S(1)} %fusion.8, f32[128,6]{0,1:T(8,128)S(1)} %bitcast.91), kind=kOutput, calls=%fused_computation.19 | convolution fusion | flops 821231616 | bytes 14358528 | tf_op jit(solution)/shard_map/hgqk,khd->qhgd/dot_general | solution.py:41
  130.9 0.2 copy.40
  131.1 0.9 convert_element_type.50
  132.0 5.7 %all-to-all-start.1 = ((bf16[8,16,768]{2,1,0:T(8,128)(2,1)}), bf16[8,16,768]{2,1,0:T(8,128)(2,1)S(1)}, u32[]{:S(2)}, u32[]{:S(2)}) async-start(bf16[8,16,768]{2,1,0:T(8,128)(2,1)} %convert_element_type.50), calls=%async_computation.1 | async-start | bytes 393216 | tf_op jit(solution)/shard_map/all_to_all | solution.py:52
  137.8 0.1 copy.43
  137.8 0.1 mul.50
  137.9 0.1 reduce_window_sum.11
  138.0 0.2 select_reduce_fusion
  138.2 76.6 %reduce-scatter.2.cloned.1.call-done = bf16[40,6144]{1,0:T(8,128)(2,1)} async-done(((bf16[1280,6144]{1,0:T(8,128)(2,1)}), bf16[40,6144]{1,0:T(8,128)(2,1)}) %reduce-scatter.2.cloned.1.call-update) | async-done | bytes 491536 | tf_op jit(solution)/shard_map/reduce_scatter | solution.py:60
  214.8 2.1 reshape.101
  216.9 0.0 all-to-all-done.1
  216.9 5.7 %all-to-all-start.2 = ((bf16[8,5,6144]{2,1,0:T(8,128)(2,1)}), bf16[8,5,6144]{2,1,0:T(8,128)(2,1)S(1)}, u32[]{:S(2)}, u32[]{:S(2)}) async-start(bf16[8,5,6144]{2,1,0:T(8,128)(2,1)} %reshape.101), calls=%async_computation.3 | async-start | bytes 1572864 | tf_op jit(solution)/shard_map/all_to_all | solution.py:67
  222.7 0.0 copy-done.4
  222.7 0.1 copy.42
  222.8 0.8 copy.45
  223.7 8.0 %all-to-all-done.2 = bf16[8,5,6144]{2,1,0:T(8,128)(2,1)S(1)} async-done(((bf16[8,5,6144]{2,1,0:T(8,128)(2,1)}), bf16[8,5,6144]{2,1,0:T(8,128)(2,1)S(1)}, u32[]{:S(2)}, u32[]{:S(2)}) %all-to-all-start.2) | async-done | bytes 491552 | tf_op jit(solution)/shard_map/all_to_all | solution.py:67
  231.7 0.2 reshape.102
  231.9 0.8 gather_fusion
  232.7 0.5 reshape.104
  233.2 1.1 multiply_reduce_fusion
  234.3 0.7 add_convert_fusion
  (9 shorter events, 0.1 us)
Async XLA Ops:
  7.2 1.3 copy-start
  7.2 207.6 %reduce-scatter.2.cloned.1.call-start = ((), (), s32[]{:S(2)}) async-start(), calls=%async_computation.4 | async-start | bytes 16220160 | tf_op jit(solution)/shard_map/reduce_scatter | solution.py:60
  22.9 0.8 copy-start.2
  22.9 13.2 %copy-start.5 = (s32[128]{0:T(128)S(1)}, s32[128]{0:T(128)}, u32[]{:S(2)}) copy-start(s32[128]{0:T(128)} %param.9) | copy-start | bytes 1540
  22.9 94.6 %copy-start.1 = (bf16[128,768]{1,0:T(8,128)(2,1)S(1)}, bf16[128,768]{1,0:T(8,128)(2,1)}, u32[]{:S(2)}) copy-start(bf16[128,768]{1,0:T(8,128)(2,1)} %param.7) | copy-start | bytes 589828
  22.9 94.8 %copy-start.3 = (s32[16,2]{0,1:T(2,128)S(1)}, s32[16,2]{0,1:T(2,128)}, u32[]{:S(2)}) copy-start(s32[16,2]{0,1:T(2,128)} %param.12) | copy-start | bytes 388
  25.4 94.5 %all-to-all-start = ((bf16[32,128,1,256]{3,1,2,0:T(8,128)(2,1)}), bf16[32,128,1,256]{3,1,2,0:T(8,128)(2,1)}, u32[]{:S(2)}, u32[]{:S(2)}) async-start(bf16[32,128,1,256]{3,1,2,0:T(8,128)(2,1)} %stack.2), calls=%async_computation | async-start | bytes 4194304 | tf_op jit(solution)/shard_map/all_to_all | solution.py:19
  126.2 96.5 %copy-start.4 = (f32[16,2]{0,1:T(2,128)S(1)}, f32[16,2]{0,1:T(2,128)}, u32[]{:S(2)}) copy-start(f32[16,2]{0,1:T(2,128)} %param.13) | copy-start | bytes 388
  132.0 84.9 %all-to-all-start.1 = ((bf16[8,16,768]{2,1,0:T(8,128)(2,1)}), bf16[8,16,768]{2,1,0:T(8,128)(2,1)S(1)}, u32[]{:S(2)}, u32[]{:S(2)}) async-start(bf16[8,16,768]{2,1,0:T(8,128)(2,1)} %convert_element_type.50), calls=%async_computation.1 | async-start | bytes 393216 | tf_op jit(solution)/shard_map/all_to_all | solution.py:52
  216.9 14.7 %all-to-all-start.2 = ((bf16[8,5,6144]{2,1,0:T(8,128)(2,1)}), bf16[8,5,6144]{2,1,0:T(8,128)(2,1)S(1)}, u32[]{:S(2)}, u32[]{:S(2)}) async-start(bf16[8,5,6144]{2,1,0:T(8,128)(2,1)} %reshape.101), calls=%async_computation.3 | async-start | bytes 1572864 | tf_op jit(solution)/shard_map/all_to_all | solution.py:67
Sparse Core Ops, SparseCore 0:
  23.1 191.6 reduce-scatter.1
